TPU v7x, 512 devices: a whole 4x8x8 slice. The times are simulated.
512 devices in a mesh: resp: 32 (over x, y), mp: 16 (over z, core).
Axes of the slice: x: 4, y: 8, z: 8, core: 2. Of those that a mesh axis runs over, the one named last changes fastest.
Arguments:
- queries: bfloat16 [32, 512, 4096], P('resp', None, 'mp'), may hold values from -160 to 160
- keys: bfloat16 [32, 512, 512], P('resp'), may hold values from -8 to 8
- values: bfloat16 [32, 512, 512], P('resp'), may hold values from -6 to 6
- out_weight: bfloat16 [4096, 8192], P(None, 'mp'), may hold values from -1.5 to 1.5
- order_bias: float32 [2, 32], replicated, may hold values from -2 to 2
- partners: int32 [32, 6], P('resp'), may hold values from -1 to 31, as said below
- count: int32 [32], P('resp'), may hold values from 1 to 6, as said below
- order: int32 [32, 6], P('resp'), may hold values 0 or 1
Outputs:
- judged: bfloat16 [32, 512, 8192], P('resp', None, 'mp')
Inputs may be any that keep to these rules, and one draw needn't show every extreme that they name: `partners`: slot s of response r is used iff s < count[r]; unused slots hold -1; a used entry names a response other than r at cyclic distance at most 3; the used entries of a row are distinct. `count`: some response has 6 partners and some other has 1.
All inputs are finite; a program needn't handle non-finite values. No bound on the sum of `order` on one device may be relied on, other than what follows from the above.
Results may differ from a plain program's by a relative error of at most 0.0057.
Values may be sent and summed in bfloat16 or wider, within the bound.
A program may use at most 64 MiB of HBM per device.

v0:
```python
import math

import jax
import jax.numpy as jnp
from jax import lax
from jax.sharding import PartitionSpec as P

HQ = 32
KVH = 4
HD = 128
REACH = 3
SLOTS = 6


def shifted(value, axis, steps):
    count = lax.axis_size(axis)
    pairs = [(source, (source + steps) % count) for source in range(count)]
    return lax.ppermute(value, axis, pairs)


def on_device(queries, keys, values, out_weight, order_bias, partners, count, order):
    seq_len = queries.shape[1]
    heads_dev = queries.shape[2] // HD
    group_size = HQ // KVH
    score_scale = 1.0 / math.sqrt(HD)
    first_head = lax.axis_index("mp") * heads_dev
    kv_head = first_head // group_size
    own_keys = lax.dynamic_slice_in_dim(keys[0], kv_head * HD, HD, 1)
    own_values = lax.dynamic_slice_in_dim(values[0], kv_head * HD, HD, 1)
    packed = jnp.stack([own_keys, own_values])
    slot_ids = jnp.arange(SLOTS, dtype=jnp.int32)
    in_use = slot_ids < count[0]
    resp_total = lax.axis_size("resp")
    resp_self = lax.axis_index("resp")
    near_offsets = list(range(1, REACH + 1)) + [-hop_id for hop_id in range(1, REACH + 1)]
    neighbours = []
    for offset in near_offsets:
        neighbours.append(shifted(packed, "resp", -offset))
    stacked = jnp.stack(neighbours)
    distance = (partners[0] - resp_self) % resp_total
    signed = jnp.where(distance <= REACH, distance, distance - resp_total)
    match = (signed[:, None] == jnp.array(near_offsets, jnp.int32)[None, :]) & in_use[:, None]
    flat = stacked.reshape(len(near_offsets), -1)
    picked = jnp.dot(match.astype(jnp.bfloat16), flat, preferred_element_type=jnp.float32)
    picked = picked.astype(jnp.bfloat16).reshape((SLOTS,) + packed.shape)
    key_rows = jnp.concatenate([own_keys[None], picked[:, 0]], 0)
    value_rows = jnp.concatenate([own_values[None], picked[:, 1]], 0)
    query_rows = queries[0].reshape(seq_len, heads_dev, HD)
    scores = (
        jnp.einsum("ihd,sjd->hisj", query_rows, key_rows, preferred_element_type=jnp.float32)
        * score_scale
    )
    bias_dev = lax.dynamic_slice_in_dim(order_bias, first_head, heads_dev, 1)
    slot_bias = jnp.where(order[0][:, None] == 1, bias_dev[1][None, :], bias_dev[0][None, :])
    bias_all = jnp.concatenate([jnp.zeros((1, heads_dev), jnp.float32), slot_bias], 0).T
    scores = scores + bias_all[:, None, :, None]
    causal = jnp.arange(seq_len)[:, None] >= jnp.arange(seq_len)[None, :]
    partner_seen = jnp.broadcast_to(in_use[None, :, None], (seq_len, SLOTS, seq_len))
    visible = jnp.concatenate([causal[:, None, :], partner_seen], 1)
    scores = jnp.where(visible[None], scores, -jnp.inf)
    highest = jnp.max(scores, axis=(2, 3), keepdims=True)
    expo = jnp.exp(scores - highest)
    weights = (expo / jnp.sum(expo, axis=(2, 3), keepdims=True)).astype(jnp.bfloat16)
    attended = jnp.einsum("hisj,sjd->ihd", weights, value_rows, preferred_element_type=jnp.float32)
    attended = attended.astype(jnp.bfloat16).reshape(seq_len, heads_dev * HD)
    judged = jnp.dot(
        lax.all_gather(attended, "mp", axis=1, tiled=True),
        out_weight,
        preferred_element_type=jnp.float32,
    )
    return judged.astype(jnp.bfloat16)[None]


def solution(mesh):
    in_specs = (
        P("resp", None, "mp"),
        P("resp", None, None),
        P("resp", None, None),
        P(None, "mp"),
        P(),
        P("resp", None),
        P("resp"),
        P("resp", None),
    )
    out_specs = P("resp", None, "mp")
    return jax.shard_map(
        on_device, mesh=mesh, in_specs=in_specs, out_specs=out_specs, check_vma=False
    )
```

profile of v0, /device:TPU:1, one launch (start us, length us, event | category | flops | bytes accessed | tf_op | source)
XLA Modules:
  0.0 158.9 jit_solution(16830722555122858521)
XLA Ops:
  6.5 1.0 constant_dynamic-slice_fusion.1
  7.6 6.1 %collective-permute-start.5 = (bf16[2,512,128]{2,1,0:T(8,128)(2,1)S(1)}, bf16[2,512,128]{2,1,0:T(8,128)(2,1)S(1)}, u32[]{:S(2)}, u32[]{:S(2)}) collective-permute-start(bf16[2,512,128]{2,1,0:T(8,128)(2,1)S(1)} %pad_maximum_fusion), channel_id=1, source_target_pairs={{0,48},{16,64},{32,80},{48,96},{64,112},{80,128},{96,144},{112,160... | collective-permute-start | bytes 786440 | tf_op jit(solution)/shard_map/ppermute | solution.py:18
  13.7 4.5 %collective-permute-start.4 = (bf16[2,512,128]{2,1,0:T(8,128)(2,1)S(1)}, bf16[2,512,128]{2,1,0:T(8,128)(2,1)S(1)}, u32[]{:S(2)}, u32[]{:S(2)}) collective-permute-start(bf16[2,512,128]{2,1,0:T(8,128)(2,1)S(1)} %pad_maximum_fusion), channel_id=1, source_target_pairs={{0,32},{16,48},{32,64},{48,80},{64,96},{80,112},{96,128},{112,144}... | collective-permute-start | bytes 786440 | tf_op jit(solution)/shard_map/ppermute | solution.py:18
  18.2 2.3 %collective-permute-start.3 = (bf16[2,512,128]{2,1,0:T(8,128)(2,1)S(1)}, bf16[2,512,128]{2,1,0:T(8,128)(2,1)S(1)}, u32[]{:S(2)}, u32[]{:S(2)}) collective-permute-start(bf16[2,512,128]{2,1,0:T(8,128)(2,1)S(1)} %pad_maximum_fusion), channel_id=1, source_target_pairs={{0,16},{16,32},{32,48},{48,64},{64,80},{80,96},{96,112},{112,128},... | collective-permute-start | bytes 786440 | tf_op jit(solution)/shard_map/ppermute | solution.py:18
  20.5 5.8 %collective-permute-start.2 = (bf16[2,512,128]{2,1,0:T(8,128)(2,1)S(1)}, bf16[2,512,128]{2,1,0:T(8,128)(2,1)S(1)}, u32[]{:S(2)}, u32[]{:S(2)}) collective-permute-start(bf16[2,512,128]{2,1,0:T(8,128)(2,1)S(1)} %pad_maximum_fusion), channel_id=1, source_target_pairs={{0,464},{16,480},{32,496},{48,0},{64,16},{80,32},{96,48},{112,64},... | collective-permute-start | bytes 786440 | tf_op jit(solution)/shard_map/ppermute | solution.py:18
  26.3 3.2 %collective-permute-start.1 = (bf16[2,512,128]{2,1,0:T(8,128)(2,1)S(1)}, bf16[2,512,128]{2,1,0:T(8,128)(2,1)S(1)}, u32[]{:S(2)}, u32[]{:S(2)}) collective-permute-start(bf16[2,512,128]{2,1,0:T(8,128)(2,1)S(1)} %pad_maximum_fusion), channel_id=1, source_target_pairs={{0,480},{16,496},{32,0},{48,16},{64,32},{80,48},{96,64},{112,80},{... | collective-permute-start | bytes 786440 | tf_op jit(solution)/shard_map/ppermute | solution.py:18
  30.4 1.9 %pad_add_fusion = pred[512,7,512]{0,2,1:T(8,128)(4,1)} fusion(pred[512,1,512]{0,2,1:T(8,128)(4,1)S(1)} %iota_compare_fusion, pred[7]{0:T(512)(128)(4,1)S(1)} %pad.4.clone), kind=kLoop, calls=%fused_computation.6 | loop fusion | flops 1835008 | bytes 2097159 | tf_op jit(solution)/shard_map/concatenate | solution.py:59
  33.0 2.6 %collective-permute-start = (bf16[2,512,128]{2,1,0:T(8,128)(2,1)S(1)}, bf16[2,512,128]{2,1,0:T(8,128)(2,1)S(1)}, u32[]{:S(2)}, u32[]{:S(2)}) collective-permute-start(bf16[2,512,128]{2,1,0:T(8,128)(2,1)S(1)} %pad_maximum_fusion), channel_id=1, source_target_pairs={{0,496},{16,0},{32,16},{48,32},{64,48},{80,64},{96,80},{112,96},{1... | collective-permute-start | bytes 786440 | tf_op jit(solution)/shard_map/ppermute | solution.py:18
  36.4 1.7 %reshape_squeeze.3 = bf16[512,2,128]{2,1,0:T(2,128)(2,1)} reshape(bf16[1,512,256]{2,1,0:T(8,128)(2,1)} %param.9) | data formatting | bytes 524288 | tf_op jit(solution)/shard_map/reshape;squeeze | solution.py:48
  38.3 5.9 %collective-permute-done.4 = bf16[2,512,128]{2,1,0:T(8,128)(2,1)S(1)} collective-permute-done((bf16[2,512,128]{2,1,0:T(8,128)(2,1)S(1)}, bf16[2,512,128]{2,1,0:T(8,128)(2,1)S(1)}, u32[]{:S(2)}, u32[]{:S(2)}) %collective-permute-start.4) | collective-permute-done | bytes 262176 | tf_op jit(solution)/shard_map/ppermute | solution.py:18
  44.3 7.6 %collective-permute-done.3 = bf16[2,512,128]{2,1,0:T(8,128)(2,1)S(1)} collective-permute-done((bf16[2,512,128]{2,1,0:T(8,128)(2,1)S(1)}, bf16[2,512,128]{2,1,0:T(8,128)(2,1)S(1)}, u32[]{:S(2)}, u32[]{:S(2)}) %collective-permute-start.3) | collective-permute-done | bytes 262176 | tf_op jit(solution)/shard_map/ppermute | solution.py:18
  51.9 0.9 stack.30
  52.8 0.9 stack.29
  53.7 2.3 %collective-permute-done.1 = bf16[2,512,128]{2,1,0:T(8,128)(2,1)S(1)} collective-permute-done((bf16[2,512,128]{2,1,0:T(8,128)(2,1)S(1)}, bf16[2,512,128]{2,1,0:T(8,128)(2,1)S(1)}, u32[]{:S(2)}, u32[]{:S(2)}) %collective-permute-start.1) | collective-permute-done | bytes 262176 | tf_op jit(solution)/shard_map/ppermute | solution.py:18
  56.0 0.9 stack.28
  56.9 3.4 %collective-permute-done = bf16[2,512,128]{2,1,0:T(8,128)(2,1)S(1)} collective-permute-done((bf16[2,512,128]{2,1,0:T(8,128)(2,1)S(1)}, bf16[2,512,128]{2,1,0:T(8,128)(2,1)S(1)}, u32[]{:S(2)}, u32[]{:S(2)}) %collective-permute-start) | collective-permute-done | bytes 262176 | tf_op jit(solution)/shard_map/ppermute | solution.py:18
  60.3 0.9 stack.27
  61.2 9.1 %stack.33 = bf16[6,131072]{1,0:T(8,128)(2,1)S(1)} concatenate(bf16[1,131072]{1,0:T(2,128)(2,1)} %stack.27, bf16[1,131072]{1,0:T(2,128)(2,1)} %stack.28, bf16[1,131072]{1,0:T(2,128)(2,1)} %stack.29, bf16[1,131072]{1,0:T(2,128)(2,1)} %stack.30, bf16[1,131072]{1,0:T(2,128)(2,1)S(1)} %stack.31, bf16[1,131072]{1,0:T(2,128)(2,1)S(1)} %stack.32), dimensions={0} | concatenate | bytes 3145728 | tf_op jit(solution)/shard_map/stack | solution.py:39
  71.3 1.0 fusion.23
  72.9 9.6 %fusion.24 = (f32[2,512]{1,0:T(2,128)S(1)}, f32[2,512,7,512]{1,3,0,2:T(8,128)}) fusion(f32[2,7]{0,1:T(8,128)S(1)} %pad_bitcast_fusion, bf16[512,2,128]{2,1,0:T(2,128)(2,1)} %reshape_squeeze.3, bf16[6,512,128]{2,1,0:T(8,128)(2,1)} %get-tuple-element.6, bf16[1,512,128]{2,1,0:T(8,128)(2,1)S(1)} %get-tuple-element.11, pred[512,7,512]{0,2,1:T(8,128)(4,1)S(1)} %copy-done.1), kind=kOutput, calls=%fused_computation.47 | convolution fusion | flops 956038144 | bytes 17698872 | tf_op jit(solution)/shard_map/ihd,sjd->hisj/dot_general | solution.py:50
  82.4 7.1 %fusion.1 = f32[2,512]{1,0:T(2,128)S(1)} fusion(f32[2,512,7,512]{1,3,0,2:T(8,128)} %get-tuple-element.10, f32[2,512]{1,0:T(2,128)S(1)} %get-tuple-element.9), kind=kLoop, calls=%fused_computation.5 | loop fusion | flops 7339008 | bytes 14688256 | tf_op jit(solution)/shard_map/reduce_sum | solution.py:63
  89.6 7.4 %fusion.6 = bf16[128,2,512]{2,0,1:T(8,128)(2,1)} fusion(f32[2,512,7,512]{1,3,0,2:T(8,128)} %get-tuple-element.10, f32[2,512]{1,0:T(2,128)S(1)} %fusion.1, f32[2,512]{1,0:T(2,128)S(1)} %get-tuple-element.9, bf16[6,512,128]{1,2,0:T(8,128)(2,1)S(1)} %bitcast.58, bf16[1,512,128]{1,2,0:T(8,128)(2,1)S(1)} %copy-done.2), kind=kOutput, calls=%fused_computation.12 | convolution fusion | flops 952500224 | bytes 15867904 | tf_op jit(solution)/shard_map/hisj,sjd->ihd/dot_general | solution.py:64
  97.0 48.4 %all-gather.2.cloned.1.call-done = bf16[512,4096]{0,1:T(8,128)(2,1)} async-done(((bf16[512,256]{0,1:T(8,128)(2,1)}), bf16[512,4096]{0,1:T(8,128)(2,1)}) %all-gather.2.cloned.1.call-update) | async-done | bytes 4194320 | tf_op jit(solution)/shard_map/all_gather | solution.py:67
  145.4 6.6 %fusion.4 = bf16[1,512,512]{2,1,0:T(8,128)(2,1)} fusion(bf16[512,4096]{0,1:T(8,128)(2,1)} %all-gather.2.cloned.1.call-done, bf16[4096,512]{1,0:T(8,128)(2,1)} %param.12), kind=kOutput, calls=%fused_computation.10 | convolution fusion | flops 2147745792 | bytes 8912896 | tf_op jit(solution)/shard_map/dot_general | solution.py:66
  (30 shorter events, 3.5 us)
Async XLA Ops:
  6.5 23.7 %copy-start = (f32[2,32]{1,0:T(2,128)S(1)}, f32[2,32]{1,0:T(2,128)}, u32[]{:S(2)}) copy-start(f32[2,32]{1,0:T(2,128)} %param.13) | copy-start | bytes 772
  6.5 31.6 %copy-start.4 = (s32[1,6]{1,0:T(1,128)S(1)}, s32[1,6]{1,0:T(1,128)}, u32[]{:S(2)}) copy-start(s32[1,6]{1,0:T(1,128)} %param.14) | copy-start | bytes 76
  6.5 138.9 %all-gather.2.cloned.1.call-start = ((), (), s32[]{:S(2)}) async-start(), calls=%async_computation | async-start | bytes 4456448 | tf_op jit(solution)/shard_map/all_gather | solution.py:67
  7.6 25.5 %collective-permute-start.5 = (bf16[2,512,128]{2,1,0:T(8,128)(2,1)S(1)}, bf16[2,512,128]{2,1,0:T(8,128)(2,1)S(1)}, u32[]{:S(2)}, u32[]{:S(2)}) collective-permute-start(bf16[2,512,128]{2,1,0:T(8,128)(2,1)S(1)} %pad_maximum_fusion), channel_id=1, source_target_pairs={{0,48},{16,64},{32,80},{48,96},{64,112},{80,128},{96,144},{112,160... | collective-permute-start | bytes 786440 | tf_op jit(solution)/shard_map/ppermute | solution.py:18
  13.7 30.5 %collective-permute-start.4 = (bf16[2,512,128]{2,1,0:T(8,128)(2,1)S(1)}, bf16[2,512,128]{2,1,0:T(8,128)(2,1)S(1)}, u32[]{:S(2)}, u32[]{:S(2)}) collective-permute-start(bf16[2,512,128]{2,1,0:T(8,128)(2,1)S(1)} %pad_maximum_fusion), channel_id=1, source_target_pairs={{0,32},{16,48},{32,64},{48,80},{64,96},{80,112},{96,128},{112,144}... | collective-permute-start | bytes 786440 | tf_op jit(solution)/shard_map/ppermute | solution.py:18
  18.2 33.7 %collective-permute-start.3 = (bf16[2,512,128]{2,1,0:T(8,128)(2,1)S(1)}, bf16[2,512,128]{2,1,0:T(8,128)(2,1)S(1)}, u32[]{:S(2)}, u32[]{:S(2)}) collective-permute-start(bf16[2,512,128]{2,1,0:T(8,128)(2,1)S(1)} %pad_maximum_fusion), channel_id=1, source_target_pairs={{0,16},{16,32},{32,48},{48,64},{64,80},{80,96},{96,112},{112,128},... | collective-permute-start | bytes 786440 | tf_op jit(solution)/shard_map/ppermute | solution.py:18
  20.5 32.3 %collective-permute-start.2 = (bf16[2,512,128]{2,1,0:T(8,128)(2,1)S(1)}, bf16[2,512,128]{2,1,0:T(8,128)(2,1)S(1)}, u32[]{:S(2)}, u32[]{:S(2)}) collective-permute-start(bf16[2,512,128]{2,1,0:T(8,128)(2,1)S(1)} %pad_maximum_fusion), channel_id=1, source_target_pairs={{0,464},{16,480},{32,496},{48,0},{64,16},{80,32},{96,48},{112,64},... | collective-permute-start | bytes 786440 | tf_op jit(solution)/shard_map/ppermute | solution.py:18
  26.3 29.7 %collective-permute-start.1 = (bf16[2,512,128]{2,1,0:T(8,128)(2,1)S(1)}, bf16[2,512,128]{2,1,0:T(8,128)(2,1)S(1)}, u32[]{:S(2)}, u32[]{:S(2)}) collective-permute-start(bf16[2,512,128]{2,1,0:T(8,128)(2,1)S(1)} %pad_maximum_fusion), channel_id=1, source_target_pairs={{0,480},{16,496},{32,0},{48,16},{64,32},{80,48},{96,64},{112,80},{... | collective-permute-start | bytes 786440 | tf_op jit(solution)/shard_map/ppermute | solution.py:18
  33.0 27.3 %collective-permute-start = (bf16[2,512,128]{2,1,0:T(8,128)(2,1)S(1)}, bf16[2,512,128]{2,1,0:T(8,128)(2,1)S(1)}, u32[]{:S(2)}, u32[]{:S(2)}) collective-permute-start(bf16[2,512,128]{2,1,0:T(8,128)(2,1)S(1)} %pad_maximum_fusion), channel_id=1, source_target_pairs={{0,496},{16,0},{32,16},{48,32},{64,48},{80,64},{96,80},{112,96},{1... | collective-permute-start | bytes 786440 | tf_op jit(solution)/shard_map/ppermute | solution.py:18
  44.3 26.0 %copy-start.3 = (s32[6]{0:T(128)S(1)}, s32[6]{0:T(128)}, u32[]{:S(2)}) copy-start(s32[6]{0:T(128)} %constant.62.clone) | copy-start | bytes 76
  71.1 1.8 %copy-start.1 = (pred[512,7,512]{0,2,1:T(8,128)(4,1)S(1)}, pred[512,7,512]{0,2,1:T(8,128)(4,1)}, u32[]{:S(2)}) copy-start(pred[512,7,512]{0,2,1:T(8,128)(4,1)} %pad_add_fusion) | copy-start | bytes 5505028
  82.4 7.1 %copy-start.2 = (bf16[1,512,128]{1,2,0:T(8,128)(2,1)S(1)}, bf16[1,512,128]{1,2,0:T(8,128)(2,1)}, u32[]{:S(2)}) copy-start(bf16[1,512,128]{1,2,0:T(8,128)(2,1)} %copy.11) | copy-start | bytes 393220
Sparse Core Ops, SparseCore 0:
  97.1 48.2 all-gather.1
where the time goes:
time: 160 us; the launch traced here: 159 us
  waiting for transfers between devices  67.6 us (42%)
  starting transfers between devices  24.5 us (15%)
  matrix products  24.4 us (15%)
  local copies, waits for them, and re-layouts  18.3 us (11%)
  between operations  14.2 us (9%)
  other arithmetic  9.86 us (6%)
    all_gather x1, waiting for transfers between devices, on_device(): lax.all_gather(attended, 'mp', axis=1, tiled=True)  48.4 us
    ppermute x6, starting transfers between devices, shifted(): return lax.ppermute(value, axis, pairs)  24.5 us
    ppermute x6, waiting for transfers between devices, shifted(): return lax.ppermute(value, axis, pairs)  19.2 us
    another operation x7, local copies, waits for them, and re-layouts, on_device(): stacked = jnp.stack(neighbours)  12.9 us
    dot_general x1, matrix products, on_device(): jnp.einsum('ihd,sjd->hisj', query_rows, key_rows, preferred_element_type=...  9.58 us
    dot_general x1, matrix products, on_device(): jnp.einsum('hisj,sjd->ihd', weights, value_rows, preferred_element_type=j...  7.41 us
    reduce_sum x1, other arithmetic, on_device(): jnp.sum(expo, axis=(2, 3), keepdims=True)  7.14 us
    dot_general x1, matrix products, on_device(): jnp.dot(lax.all_gather(attended, 'mp', axis=1, tiled=True), out_weight, p...  6.61 us
  transfers between devices with their start and end apart: 7, of which 5 were waited for; matrix products, arithmetic and copies ran while one was open for 5% of the time, Pallas kernels for 0%

commit v1 on v0

v1 whole, which is shorter than its diff:
```python
import functools
import math

import jax
import jax.numpy as jnp
from jax import lax
from jax.experimental import pallas as pl
from jax.experimental.pallas import tpu as pltpu
from jax.sharding import PartitionSpec as P

HQ = 32
KVH = 4
HD = 128
REACH = 3
SLOTS = 6
LEN = 512
ROWS = 256
ONES = 16
MESH = pl.DeviceIdType.MESH
LOG2E = math.log2(math.e)
ABSENT = -1e30


def kernel(
    nr,
    nm,
    partners_ref,
    count_ref,
    order_ref,
    bias_ref,
    q_hbm,
    k_hbm,
    v_hbm,
    w_hbm,
    out_hbm,
    qs,
    kv,
    vraw,
    w,
    g,
    acc,
    o_acc,
    m_acc,
    outv,
    load_sem,
    kv_send,
    kv_recv,
    kvs_send,
    kvs_recv,
    g_send,
    g_recv,
    gs_send,
    gs_recv,
    out_sem,
):
    resp = lax.axis_index("resp")
    mp = lax.axis_index("mp")
    core = lax.rem(mp, 2)
    other = 1 - core
    kv_head = lax.div(mp * 2, HQ // KVH)
    r_next, r_prev = lax.rem(resp + 1, nr), lax.rem(resp + nr - 1, nr)
    z_next, z_prev = lax.rem(mp + 2, nm), lax.rem(mp + nm - 2, nm)
    sib = mp + 1 - 2 * core
    half_len = LEN // 2
    scale = LOG2E / math.sqrt(HD)

    columns = pl.ds(pl.multiple_of(kv_head * HD, HD), HD)
    load_k = pltpu.make_async_copy(k_hbm.at[0, :, columns], kv.at[0, 0], load_sem.at[0])
    load_v = pltpu.make_async_copy(v_hbm.at[0, :, columns], vraw, load_sem.at[1])
    load_v.start()
    load_k.start()
    load_q = []
    for chunk in range(4):
        head, part = chunk // 2, chunk % 2
        load_q.append(
            pltpu.make_async_copy(
                q_hbm.at[0, pl.ds(part * ROWS, ROWS), pl.ds(head * HD, HD)],
                qs.at[chunk],
                load_sem.at[2 + chunk],
            )
        )
        load_q[-1].start()
    load_w = pltpu.make_async_copy(w_hbm, w, load_sem.at[6])
    load_w.start()

    barrier = pltpu.get_barrier_semaphore()
    for device in ((r_next, mp), (r_prev, mp), (resp, z_next), (resp, z_prev), (resp, sib)):
        pl.semaphore_signal(barrier, inc=1, device_id=device, device_id_type=MESH)

    load_v.wait()
    for block in range(LEN // HD):
        rows = pl.ds(block * HD, HD)
        kv[0, 1, rows, :] = vraw[rows, :].T
    load_k.wait()
    pl.semaphore_wait(barrier, 5)

    def kv_copy(step, way, half):
        source = 0 if step == 1 else 1 + 2 * (step - 2) + way
        target = 1 + 2 * (step - 1) + way
        rows = pl.ds(half * half_len, half_len)
        index = (2 * (step - 1) + way) * 2 + half
        return pltpu.make_async_remote_copy(
            src_ref=kv.at[source, core, rows],
            dst_ref=kv.at[target, core, rows],
            send_sem=kv_send.at[index],
            recv_sem=kv_recv.at[index],
            device_id=((r_next, r_prev)[way], mp),
            device_id_type=MESH,
        )

    def kv_share(step, way, half, which):
        slot = 1 + 2 * (step - 1) + way
        rows = pl.ds(half * half_len, half_len)
        index = (2 * (step - 1) + way) * 2 + half
        return pltpu.make_async_remote_copy(
            src_ref=kv.at[slot, which, rows],
            dst_ref=kv.at[slot, which, rows],
            send_sem=kvs_send.at[index],
            recv_sem=kvs_recv.at[index],
            device_id=(resp, sib),
            device_id_type=MESH,
        )

    for half in range(2):
        for way in range(2):
            kv_copy(1, way, half).start()

    def pass_on(step, half):
        for way in range(2):
            kv_copy(step, way, half).wait_recv()
            if step < REACH:
                kv_copy(step + 1, way, half).start()
            kv_share(step, way, half, core).start()

    def from_sibling(step):
        for half in range(2):
            for way in range(2):
                kv_share(step, way, half, other).wait_recv()

    def offset_bias(step, way, head):
        name = lax.rem(resp + (nr - step if way == 0 else step), nr)
        low = bias_ref[0, 2 * mp + head] * LOG2E
        high = bias_ref[1, 2 * mp + head] * LOG2E
        result = jnp.float32(ABSENT)
        for slot in range(SLOTS):
            listed = (partners_ref[0, slot] == name) & (slot < count_ref[0])
            result = jnp.where(listed, jnp.where(order_ref[0, slot] == 1, high, low), result)
        return result

    def transposed_values(slot):
        blocks = [kv[slot, 1, pl.ds(b * HD, HD), :] for b in range(LEN // HD)]
        joined = jnp.concatenate(blocks, axis=1)
        return jnp.concatenate([joined, jnp.ones((ONES, LEN), jnp.bfloat16)], axis=0)

    def scores(keys, queries):
        return lax.dot_general(
            keys, queries, (((1,), (1,)), ((), ())), preferred_element_type=jnp.float32
        )

    for copy in load_q:
        copy.wait()

    def own_block(chunk, part):
        length = (part + 1) * ROWS
        s = scores(kv[0, 0, pl.ds(0, length), :], qs[chunk]) * scale
        key_pos = lax.broadcasted_iota(jnp.int32, (length, ROWS), 0)
        query_pos = lax.broadcasted_iota(jnp.int32, (length, ROWS), 1) + part * ROWS
        s = jnp.where(key_pos <= query_pos, s, ABSENT)
        top = jnp.max(s, axis=0, keepdims=True)
        p = jnp.exp2(s - top).astype(jnp.bfloat16)
        vt = transposed_values(0)[:, :length]
        m_acc[chunk] = jnp.broadcast_to(top, (8, ROWS))
        o_acc[chunk] = jnp.dot(vt, p, preferred_element_type=jnp.float32)

    def pair_block(step, chunk, bias0, bias1):
        first = 1 + 2 * (step - 1)
        queries = qs[chunk]
        s0 = scores(kv[first, 0], queries) * scale
        s1 = scores(kv[first + 1, 0], queries) * scale
        before = m_acc[chunk, 0:1, :]
        top = jnp.maximum(
            jnp.max(s0, axis=0, keepdims=True) + bias0, jnp.max(s1, axis=0, keepdims=True) + bias1
        )
        top = jnp.maximum(before, top)
        p0 = jnp.exp2(s0 - (top - bias0)).astype(jnp.bfloat16)
        p1 = jnp.exp2(s1 - (top - bias1)).astype(jnp.bfloat16)
        fresh = jnp.dot(transposed_values(first), p0, preferred_element_type=jnp.float32)
        fresh += jnp.dot(transposed_values(first + 1), p1, preferred_element_type=jnp.float32)
        m_acc[chunk] = jnp.broadcast_to(top, (8, ROWS))
        o_acc[chunk] = o_acc[chunk] * jnp.exp2(before - top) + fresh

    def finish(chunk):
        head, part = chunk // 2, chunk % 2
        total = o_acc[chunk]
        normal = total[:HD, :] * (1.0 / total[HD : HD + 1, :])
        g[2 * mp + head, pl.ds(part * ROWS, ROWS), :] = normal.T.astype(jnp.bfloat16)

    for chunk in range(4):
        own_block(chunk, chunk % 2)

    chips = nm // 2
    reach = (chips // 2, chips - 1 - chips // 2)

    def hops(way, head):
        return reach[0] if way == head else reach[1]

    def origin(way, hop):
        return lax.rem(mp + (nm - 2 * hop if way == 0 else 2 * hop), nm)

    def g_copy(hop, way, head):
        row = 2 * origin(way, hop - 1) + head
        index = ((hop - 1) * 2 + way) * 2 + head
        return pltpu.make_async_remote_copy(
            src_ref=g.at[row],
            dst_ref=g.at[row],
            send_sem=g_send.at[index],
            recv_sem=g_recv.at[index],
            device_id=(resp, (z_next, z_prev)[way]),
            device_id_type=MESH,
        )

    def g_arrival(hop, way, head):
        row = 2 * origin(way, hop) + head
        index = ((hop - 1) * 2 + way) * 2 + head
        return pltpu.make_async_remote_copy(
            src_ref=g.at[row],
            dst_ref=g.at[row],
            send_sem=g_send.at[index],
            recv_sem=g_recv.at[index],
            device_id=(resp, (z_next, z_prev)[way]),
            device_id_type=MESH,
        )

    def g_share(hop, way, head, sent):
        row = 2 * origin(way, hop) + head
        row = row if sent else row + 2 * (sib - mp)
        index = (hop * 2 + way) * 2 + head
        return pltpu.make_async_remote_copy(
            src_ref=g.at[row],
            dst_ref=g.at[row],
            send_sem=gs_send.at[index],
            recv_sem=gs_recv.at[index],
            device_id=(resp, sib),
            device_id_type=MESH,
        )

    for step in range(1, REACH + 1):
        pass_on(step, 0)
        pass_on(step, 1)
        from_sibling(step)
        for head in range(2):
            bias0, bias1 = offset_bias(step, 0, head), offset_bias(step, 1, head)
            for part in range(2):
                pair_block(step, head * 2 + part, bias0, bias1)
                if step == REACH:
                    finish(head * 2 + part)
            if step == REACH:
                g_copy(1, 0, head).start()
                g_copy(1, 1, head).start()
                g_share(0, 0, head, True).start()

    load_w.wait()

    def product(device, rows):
        left = jnp.concatenate([g[2 * device, rows, :], g[2 * device + 1, rows, :]], axis=1)
        right = w[pl.ds(pl.multiple_of(device * 2 * HD, 2 * HD), 2 * HD), :]
        return jnp.dot(left, right, preferred_element_type=jnp.float32)

    def add_product(device, first=False):
        for part in range(2):
            rows = pl.ds(part * ROWS, ROWS)
            if first:
                acc[rows, :] = product(device, rows)
            else:
                acc[rows, :] += product(device, rows)

    add_product(mp, True)
    pending = [(0, 0)]
    for hop in range(1, reach[0] + 1):
        later = []
        for head in range(2):
            for way in range(2):
                if hop > hops(way, head):
                    continue
                g_arrival(hop, way, head).wait_recv()
                if hop < hops(way, head):
                    g_copy(hop + 1, way, head).start()
                g_share(hop, way, head, True).start()
        if hop < reach[0]:
            for way, back in pending:
                for head in range(2):
                    g_share(back, way, head, False).wait_recv()
                add_product(origin(way, back) + sib - mp)
            for way in range(2):
                add_product(origin(way, hop))
            pending = [(0, hop), (1, hop)]
    for way, back in pending:
        for head in range(2):
            g_share(back, way, head, False).wait_recv()
        add_product(origin(way, back) + sib - mp)
    add_product(origin(0, reach[0]))
    for way in range(2):
        g_share(reach[0], way, way, False).wait_recv()
    last = origin(0, reach[0]) + sib - mp
    stores = []
    for part in range(2):
        rows = pl.ds(part * ROWS, ROWS)
        outv[rows, :] = (acc[rows, :] + product(last, rows)).astype(jnp.bfloat16)
        stores.append(pltpu.make_async_copy(outv.at[rows], out_hbm.at[0, rows], out_sem.at[part]))
        stores[-1].start()

    for step in range(1, REACH + 1):
        for half in range(2):
            for way in range(2):
                kv_copy(step, way, half).wait_send()
                kv_share(step, way, half, core).wait_send()
    for head in range(2):
        g_share(0, 0, head, True).wait_send()
        for way in range(2):
            for hop in range(1, hops(way, head) + 1):
                g_copy(hop, way, head).wait_send()
                g_share(hop, way, head, True).wait_send()
    for copy in stores:
        copy.wait()


def on_device(queries, keys, values, out_weight, order_bias, partners, count, order):
    nr, nm = lax.axis_size("resp"), lax.axis_size("mp")
    smem = pl.BlockSpec(memory_space=pltpu.SMEM)
    anywhere = pl.BlockSpec(memory_space=pl.ANY)
    seq_len = queries.shape[1]
    width = out_weight.shape[1]
    kv_copies = 4 * REACH
    hop_copies = 4 * (nm // 4)
    return pl.pallas_call(
        functools.partial(kernel, nr, nm),
        out_shape=jax.ShapeDtypeStruct((1, seq_len, width), jnp.bfloat16),
        in_specs=[smem] * 4 + [anywhere] * 4,
        out_specs=anywhere,
        scratch_shapes=[
            pltpu.VMEM((4, ROWS, HD), jnp.bfloat16),
            pltpu.VMEM((1 + 2 * REACH, 2, LEN, HD), jnp.bfloat16),
            pltpu.VMEM((LEN, HD), jnp.bfloat16),
            pltpu.VMEM(out_weight.shape, jnp.bfloat16),
            pltpu.VMEM((HQ, LEN, HD), jnp.bfloat16),
            pltpu.VMEM((seq_len, width), jnp.float32),
            pltpu.VMEM((4, HD + ONES, ROWS), jnp.float32),
            pltpu.VMEM((4, 8, ROWS), jnp.float32),
            pltpu.VMEM((seq_len, width), jnp.bfloat16),
            pltpu.SemaphoreType.DMA((7,)),
            pltpu.SemaphoreType.DMA((kv_copies,)),
            pltpu.SemaphoreType.DMA((kv_copies,)),
            pltpu.SemaphoreType.DMA((kv_copies,)),
            pltpu.SemaphoreType.DMA((kv_copies,)),
            pltpu.SemaphoreType.DMA((hop_copies,)),
            pltpu.SemaphoreType.DMA((hop_copies,)),
            pltpu.SemaphoreType.DMA((hop_copies + 4,)),
            pltpu.SemaphoreType.DMA((hop_copies + 4,)),
            pltpu.SemaphoreType.DMA((2,)),
        ],
        compiler_params=pltpu.CompilerParams(
            collective_id=0, has_side_effects=True, vmem_limit_bytes=56 * 1024 * 1024
        ),
    )(partners, count, order, order_bias, queries, keys, values, out_weight)


def solution(mesh):
    in_specs = (
        P("resp", None, "mp"),
        P("resp", None, None),
        P("resp", None, None),
        P(None, "mp"),
        P(),
        P("resp", None),
        P("resp"),
        P("resp", None),
    )
    out_specs = P("resp", None, "mp")
    return jax.shard_map(
        on_device, mesh=mesh, in_specs=in_specs, out_specs=out_specs, check_vma=False
    )
```

time: 160 us -> 61.2 us (0.38)
  waiting for transfers between devices: 67.6 us -> 0 us
  Pallas kernels: 0 us -> 58.5 us
  starting transfers between devices: 24.5 us -> 0 us
  matrix products: 24.4 us -> 0 us
  local copies, waits for them, and re-layouts: 18.3 us -> 1.87 us
  between operations: 14.2 us -> 0.66 us
  other arithmetic: 9.86 us -> 0 us
    pallas_call x0 -> x1, Pallas kernels: none -> 58.5 us  [on_device(): pl.pallas_call(functools.partial(kernel, nr, nm), out_shape=jax.ShapeDtyp...]
    all_gather x1 -> x0, waiting for transfers between devices: 48.4 us -> none  [on_device(): lax.all_gather(attended, 'mp', axis=1, tiled=True)]
    ppermute x6 -> x0, starting transfers between devices: 24.5 us -> none  [shifted(): return lax.ppermute(value, axis, pairs)]
    dot_general x4 -> x0, matrix products: 24.4 us -> none  [the longest x1 9.58 us: on_device(): jnp.einsum('ihd,sjd->hisj', query_rows, key_rows, preferred_element_type=...]
    ppermute x6 -> x0, waiting for transfers between devices: 19.2 us -> none  [shifted(): return lax.ppermute(value, axis, pairs)]
    another operation x8 -> x0, local copies, waits for them, and re-layouts: 14.6 us -> none  [the longest x7 12.9 us: on_device(): stacked = jnp.stack(neighbours)]
    reduce_sum x1 -> x0, other arithmetic: 7.14 us -> none  [on_device(): jnp.sum(expo, axis=(2, 3), keepdims=True)]
    concatenate x1 -> x0, other arithmetic: 1.86 us -> none  [on_device(): visible = jnp.concatenate([causal[:, None, :], partner_seen], 1)]
  transfers between devices with their start and end apart: 7 -> 0, of which waited for: 5 -> 0; matrix products, arithmetic and copies ran while one was open for 5% -> 0% of each run, Pallas kernels for 0% -> 0%
where the time goes in v1:
time: 61.2 us; the launch traced here: 61 us
  Pallas kernels  58.5 us (96%)
  local copies, waits for them, and re-layouts  1.87 us (3%)
  between operations  0.66 us (1%)
    pallas_call x1, Pallas kernels, on_device(): pl.pallas_call(functools.partial(kernel, nr, nm), out_shape=jax.ShapeDtyp...  58.5 us
    unnamed x1, local copies, waits for them, and re-layouts  1.87 us

profile of v1, /device:TPU:1, one launch (start us, length us, event | category | flops | bytes accessed | tf_op | source)
XLA Modules:
  0.0 61.0 jit_solution(9698516071152585770)
XLA Ops:
  0.7 58.5 %shard_map.82 = bf16[1,512,512]{2,1,0:T(8,128)(2,1)} custom-call(s32[1,6]{1,0:T(1,128)} %partners_ref.1, s32[1]{0:T(128)S(6)} %copy.10.count_ref, s32[1,6]{1,0:T(1,128)} %order_ref.1, f32[2,32]{1,0:T(2,128)} %bias_ref.1, bf16[1,512,256]{2,1,0:T(8,128)(2,1)} %q_hbm.1, bf16[1,512,512]{2,1,0:T(8,128)(2,1)} %k_hbm.1, bf16[1,512,512]{2,1,0:T(8,128)(2,1)} %v_hbm.1, ...), custom_call_target="tpu_custom_call" | custom-call | tf_op jit(solution)/shard_map/pallas_call | solution.py:335
  59.2 1.9 %copy.11 = bf16[1,512,512]{2,1,0:T(8,128)(2,1)} copy(bf16[1,512,512]{2,1,0:T(8,128)(2,1)} %shard_map.82) | data formatting | bytes 1048576
